TPU v7x, 32 devices: a whole 2x2x4 slice. The times are simulated.
32 devices in a mesh: dom: 32 (over z, y, x, core).
Axes of the slice: x: 2, y: 2, z: 4, core: 2. Of those that a mesh axis runs over, the one named last changes fastest.
Arguments:
- entities: float32 [32768, 200], P('dom'), may hold values from -3 to 3
- entity_state: float32 [32768], P('dom'), may hold values from 1e-05 to 0.1
- relations: float32 [1345, 200], replicated, may hold values from -3 to 3
- relation_state: float32 [1345], replicated, may hold values from 1 to 100
- edges: int32 [2, 3, 16384], P(None, None, 'dom'), may hold values from 0 to 1344, as said below
- negatives: int32 [2, 128, 1000], P(None, 'dom'), may hold values from 0 to 1023
- counts: int32 [2, 32], P(None, 'dom'), may hold values from 1 to 512, as said below
Outputs:
- entities_after: float32 [32768, 200], P('dom')
- entity_state_after: float32 [32768], P('dom')
- relations_after: float32 [1345, 200], replicated
- relation_state_after: float32 [1345], replicated
Inputs may be any that keep to these rules, and one draw needn't show every extreme that they name: `edges`: rows 0 and 2 are local entity ids below 1024; row 1 holds relation ids below 1345. `negatives`: local ids in the partner's partition. `counts`: in every round some bucket is full.
All inputs are finite; a program needn't handle non-finite values.
Results may differ from a plain program's by a relative error of at most 0.0003.
Values sent between devices are 32-bit elements; how exact they have to be, the bound alone decides.
A program may use at most 64 MiB of HBM per device.

v0:
```python
import jax
import jax.numpy as jnp
from jax import lax
from jax.sharding import PartitionSpec as P

RATE = 0.2
HIGH = lax.Precision.HIGHEST


def swapped(block, axis, apart):
    count = lax.axis_size(axis)
    route = []
    for low in range(count):
        high = low | 1 << apart
        if high != low and high < count:
            route += [(low, high), (high, low)]
    return lax.ppermute(block, axis, route)


def block_terms(carry, table, relations, source, relation, target, negative_ids, live):
    grad_table, grad_relation = carry
    half = table.shape[1] // 2
    src_rows = table[source]
    tgt_rows = table[target]
    neg_rows = table[negative_ids]
    rel_rows = relations[relation]
    src_real, src_imag = (src_rows[:, :half], src_rows[:, half:])
    rel_real, rel_imag = (rel_rows[:, :half], rel_rows[:, half:])
    product = jnp.concatenate(
        [src_real * rel_real - src_imag * rel_imag, src_real * rel_imag + src_imag * rel_real],
        axis=1,
    )
    positive = jnp.sum(product * tgt_rows, axis=1)
    negative = lax.dot_general(
        product,
        neg_rows,
        (((1,), (1,)), ((), ())),
        precision=HIGH,
        preferred_element_type=jnp.float32,
    )
    pos_weight = -jax.nn.sigmoid(-positive) * live
    neg_weight = jax.nn.sigmoid(negative) * (live[:, None] / negative.shape[1])
    upstream = pos_weight[:, None] * tgt_rows + jnp.dot(
        neg_weight, neg_rows, precision=HIGH, preferred_element_type=jnp.float32
    )
    target_grad = pos_weight[:, None] * product
    negative_grad = lax.dot_general(
        neg_weight,
        product,
        (((0,), (0,)), ((), ())),
        precision=HIGH,
        preferred_element_type=jnp.float32,
    )
    up_real, up_imag = (upstream[:, :half], upstream[:, half:])
    source_grad = jnp.concatenate(
        [up_real * rel_real + up_imag * rel_imag, up_imag * rel_real - up_real * rel_imag], axis=1
    )
    relation_grad = jnp.concatenate(
        [up_real * src_real + up_imag * src_imag, up_imag * src_real - up_real * src_imag], axis=1
    )
    grad_table = (
        grad_table.at[source]
        .add(source_grad)
        .at[target]
        .add(target_grad)
        .at[negative_ids]
        .add(negative_grad)
    )
    grad_relation = grad_relation.at[relation].add(relation_grad)
    return (grad_table, grad_relation)


def bucket_pass(
    carry,
    table,
    relations,
    edge_pair,
    negative_pair,
    count_pair,
    source_shift,
    target_shift,
    block,
    first,
    last,
):
    block_pair = (count_pair + block - 1) // block

    def visit(index, inner):
        which = (index >= block_pair[0]).astype(jnp.int32)
        number = index - which * block_pair[0]
        edge_list = lax.dynamic_index_in_dim(edge_pair, which, 0, keepdims=False)
        start = number * block
        window = lax.dynamic_slice_in_dim(edge_list, start, block, 1)
        negative_list = lax.dynamic_index_in_dim(negative_pair, which, 0, keepdims=False)
        negative_ids = (
            lax.dynamic_index_in_dim(negative_list, number, 0, keepdims=False) + target_shift[which]
        )
        live = (start + jnp.arange(block, dtype=jnp.int32) < count_pair[which]).astype(jnp.float32)
        return block_terms(
            inner,
            table,
            relations,
            window[0] + source_shift[which],
            window[1],
            window[2] + target_shift[which],
            negative_ids,
            live,
        )

    return lax.fori_loop(first, last, visit, carry)


def adagrad(param, state, grad):
    new_state = state + jnp.mean(grad * grad, axis=1)
    return (param - RATE * grad / jnp.sqrt(new_state)[:, None], new_state)


def body(entities, entity_state, relations, relation_state, edges, negatives, counts):
    rows = entities.shape[0]
    blocks_dev = negatives.shape[1]
    block = edges.shape[2] // blocks_dev
    levels = lax.axis_size("dom").bit_length() - 1
    for round_index, bit in enumerate((levels - 1, 0)):
        partner = swapped(entities, "dom", bit)
        table = jnp.concatenate([entities, partner], axis=0)
        own_edges = edges[round_index]
        own_negatives = negatives[round_index]
        own_count = counts[round_index]
        other_edges, other_negatives, other_count = swapped(
            (own_edges, own_negatives, own_count), "dom", bit
        )
        upper = lax.axis_index("dom") // 2**bit % 2
        flipped = upper == 1
        edge_pair = jnp.where(
            flipped, jnp.stack([other_edges, own_edges]), jnp.stack([own_edges, other_edges])
        )
        negative_pair = jnp.where(
            flipped,
            jnp.stack([other_negatives, own_negatives]),
            jnp.stack([own_negatives, other_negatives]),
        )
        count_pair = jnp.where(
            flipped,
            jnp.concatenate([other_count, own_count]),
            jnp.concatenate([own_count, other_count]),
        )
        source_shift = jnp.stack([upper * rows, (1 - upper) * rows])
        target_shift = jnp.stack([(1 - upper) * rows, upper * rows])
        block_pair = (count_pair + block - 1) // block
        total = block_pair[0] + block_pair[1]
        middle = (total + 1) // 2
        first = upper * middle
        last = middle + upper * (total - middle)
        empty = (
            jnp.zeros((2 * rows, entities.shape[1]), jnp.float32),
            jnp.zeros(relations.shape, jnp.float32),
        )
        grads, relation_grads = bucket_pass(
            empty,
            table,
            relations,
            edge_pair,
            negative_pair,
            count_pair,
            source_shift,
            target_shift,
            block,
            first,
            last,
        )
        returned = swapped(grads[rows:], "dom", bit)
        relation_total = lax.psum(relation_grads, "dom")
        entities, entity_state = adagrad(entities, entity_state, grads[:rows] + returned)
        relations, relation_state = adagrad(relations, relation_state, relation_total)
    return (entities, entity_state, relations, relation_state)


def solution(mesh):
    return jax.shard_map(
        body,
        mesh=mesh,
        in_specs=(
            P("dom", None),
            P("dom"),
            P(),
            P(),
            P(None, None, "dom"),
            P(None, "dom", None),
            P(None, "dom"),
        ),
        out_specs=(P("dom", None), P("dom"), P(), P()),
        check_vma=False,
    )
```

profile of v0, /device:TPU:0, one launch (start us, length us, event | category | flops | bytes accessed | tf_op | source)
XLA Modules:
  0.0 609.5 jit_solution(12843747475687905343)
XLA Ops:
  8.5 4.1 collective-permute-start
  14.0 2.9 collective-permute-start.1
  18.3 2.8 copy.91
  24.3 27.5 %collective-permute-done.1 = s32[3,512]{1,0:T(4,128)S(1)} collective-permute-done((s32[3,512]{1,0:T(4,128)S(1)}, s32[3,512]{1,0:T(4,128)S(1)}, u32[]{:S(2)}, u32[]{:S(2)}) %collective-permute-start.1) | collective-permute-done | bytes 6176 | tf_op jit(solution)/shard_map/ppermute | solution.py:17
  55.3 80.7 %while.30 = (s32[]{:T(128)}, f32[2048,200]{1,0:T(8,128)S(1)}, f32[1345,200]{1,0:T(8,128)}, s32[]{:T(128)}, s32[2]{0:T(128)S(1)}, /*index=5*/s32[2,3,512]{2,1,0:T...) while((s32[]{:T(128)}, f32[2048,200]{1,0:T(8,128)S(1)}, ...), condition=%wide.region_6.7_spmd, body=%wide.region_0.6_spmd.sunk | while | flops 922911104 | bytes 17251100 | solution.py:110
  59.4 2.1 gather_fusion.3
  61.8 2.4 gather_fusion.2
  64.3 2.3 gather_fusion
  68.3 5.2 gather_fusion.1
  78.6 2.0 fusion.66
  80.7 4.0 scatter_fusion.3
  84.6 2.0 scatter_fusion
  86.7 2.0 scatter_fusion.1
  88.8 6.8 %scatter_fusion.2 = f32[2048,200]{1,0:T(8,128)S(1)} fusion(f32[2048,200]{1,0:T(8,128)S(1)} %scatter_fusion.1, s32[1000]{0:T(1024)S(1)} %bitcast.123, f32[1000,200]{1,0:T(8,128)S(1)} %fusion.66), kind=kCustom, calls=%fused_computation.10.clone.1 | custom fusion | flops 200000 | bytes 2404000 | tf_op jit(solution)/shard_map/while/body/scatter-add | solution.py:67
  99.7 2.1 gather_fusion.3
  102.2 2.4 gather_fusion.2
  104.6 2.3 gather_fusion
  108.6 5.2 gather_fusion.1
  121.0 4.0 scatter_fusion.3
  125.0 2.0 scatter_fusion
  127.0 2.0 scatter_fusion.1
  129.1 6.8 %scatter_fusion.2 = f32[2048,200]{1,0:T(8,128)S(1)} fusion(f32[2048,200]{1,0:T(8,128)S(1)} %scatter_fusion.1, s32[1000]{0:T(1024)S(1)} %bitcast.123, f32[1000,200]{1,0:T(8,128)S(1)} %fusion.66), kind=kCustom, calls=%fused_computation.10.clone.1 | custom fusion | flops 200000 | bytes 2404000 | tf_op jit(solution)/shard_map/while/body/scatter-add | solution.py:67
  137.8 2.2 slice.233
  148.7 19.3 %collective-permute-done.4 = f32[1024,200]{0,1:T(8,128)} collective-permute-done((f32[1024,200]{0,1:T(8,128)}, f32[1024,200]{0,1:T(8,128)}, u32[]{:S(2)}, u32[]{:S(2)}) %collective-permute-start.4) | collective-permute-done | bytes 819232 | tf_op jit(solution)/shard_map/ppermute | solution.py:17
  169.3 2.3 divide_subtract_fusion.3
  171.6 147.5 %all-reduce.3.cloned.1.call-done = f32[1345,200]{0,1:T(8,128)} async-done(((f32[1345,200]{0,1:T(8,128)}), f32[1345,200]{0,1:T(8,128)}) %all-reduce.3.cloned.1.call-update) | async-done | bytes 1076016 | tf_op jit(solution)/shard_map/psum | solution.py:172
  328.1 89.5 %while.31 = (s32[]{:T(128)}, f32[2048,200]{1,0:T(8,128)S(1)}, f32[1345,200]{1,0:T(8,128)}, s32[]{:T(128)}, s32[2]{0:T(128)}, /*index=5*/s32[2,3,512]{2,1,0:T(4,1...) while((s32[]{:T(128)}, f32[2048,200]{1,0:T(8,128)S(1)}, ...), condition=%wide.region_16.17_spmd, body=%wide.region_10.16_spmd.sunk | while | flops 922911104 | bytes 16896204 | solution.py:110
  336.8 2.1 gather_fusion.7
  339.2 2.4 gather_fusion.6
  341.7 2.3 gather_fusion.4
  345.7 5.2 gather_fusion.5
  356.0 2.0 fusion.75
  358.0 4.0 scatter_fusion.7
  362.0 2.0 scatter_fusion.4
  364.0 2.0 scatter_fusion.5
  366.1 6.8 %scatter_fusion.6 = f32[2048,200]{1,0:T(8,128)S(1)} fusion(f32[2048,200]{1,0:T(8,128)S(1)} %scatter_fusion.5, s32[1000]{0:T(1024)S(1)} %bitcast.125, f32[1000,200]{1,0:T(8,128)S(1)} %fusion.75), kind=kCustom, calls=%fused_computation.14.clone.1 | custom fusion | flops 200000 | bytes 2404000 | tf_op jit(solution)/shard_map/while/body/scatter-add | solution.py:67
  381.4 2.1 gather_fusion.7
  383.8 2.4 gather_fusion.6
  386.3 2.3 gather_fusion.4
  390.3 5.2 gather_fusion.5
  400.6 2.0 fusion.75
  402.7 4.0 scatter_fusion.7
  406.6 2.0 scatter_fusion.4
  408.7 2.0 scatter_fusion.5
  410.7 6.8 %scatter_fusion.6 = f32[2048,200]{1,0:T(8,128)S(1)} fusion(f32[2048,200]{1,0:T(8,128)S(1)} %scatter_fusion.5, s32[1000]{0:T(1024)S(1)} %bitcast.125, f32[1000,200]{1,0:T(8,128)S(1)} %fusion.75), kind=kCustom, calls=%fused_computation.14.clone.1 | custom fusion | flops 200000 | bytes 2404000 | tf_op jit(solution)/shard_map/while/body/scatter-add | solution.py:67
  417.6 2.8 copy.100
  423.5 172.2 %all-reduce.5.cloned.1.call-done = f32[1345,200]{0,1:T(8,128)} async-done(((f32[1345,200]{0,1:T(8,128)}), f32[1345,200]{0,1:T(8,128)}) %all-reduce.5.cloned.1.call-update) | async-done | bytes 1076016 | tf_op jit(solution)/shard_map/psum | solution.py:172
  600.4 2.3 divide_subtract_fusion.2
  (315 shorter events, 88.7 us)
Async XLA Ops:
  7.2 44.9 %copy-start.23 = (f32[1024,200]{0,1:T(8,128)S(1)}, f32[1024,200]{0,1:T(8,128)}, u32[]{:S(2)}) copy-start(f32[1024,200]{0,1:T(8,128)} %param.11) | copy-start | bytes 2457604
  7.2 311.9 %all-reduce.3.cloned.1.call-start = ((), (), s32[]{:S(2)}) async-start(), calls=%async_computation | async-start | bytes 2252800 | tf_op jit(solution)/shard_map/psum | solution.py:172
  8.5 12.6 %collective-permute-start = (s32[1]{0:T(128)}, s32[1]{0:T(128)}, u32[]{:S(2)}, u32[]{:S(2)}) collective-permute-start(s32[1]{0:T(128)} %bitcast.24), channel_id=1, source_target_pairs={{0,16},{16,0},{1,17},{17,1},{2,18},{18,2},{3,19},{19,3},{4,20},{20... | collective-permute-start | bytes 20 | tf_op jit(solution)/shard_map/ppermute | solution.py:17
  12.6 39.4 %collective-permute-start.2 = (f32[1024,200]{0,1:T(8,128)}, f32[1024,200]{0,1:T(8,128)S(1)}, u32[]{:S(2)}, u32[]{:S(2)}) collective-permute-start(f32[1024,200]{0,1:T(8,128)} %param.11), channel_id=1, source_target_pairs={{0,16},{16,0},{1,17},{17,1},{2,18},{18,2},{3,19},{19,3},{4,20},{20... | collective-permute-start | bytes 2457608 | tf_op jit(solution)/shard_map/ppermute | solution.py:17
  14.0 37.8 %collective-permute-start.1 = (s32[3,512]{1,0:T(4,128)S(1)}, s32[3,512]{1,0:T(4,128)S(1)}, u32[]{:S(2)}, u32[]{:S(2)}) collective-permute-start(s32[3,512]{1,0:T(4,128)S(1)} %bitcast.126), channel_id=1, source_target_pairs={{0,16},{16,0},{1,17},{17,1},{2,18},{18,2},{3,19},{19,3},{4,20},{20... | collective-permute-start | bytes 18440 | tf_op jit(solution)/shard_map/ppermute | solution.py:17
  18.3 33.8 %collective-permute-start.3 = (s32[4,1000]{1,0:T(4,128)S(1)}, s32[4,1000]{1,0:T(4,128)S(1)}, u32[]{:S(2)}, u32[]{:S(2)}) collective-permute-start(s32[4,1000]{1,0:T(4,128)S(1)} %get-tuple-element.543), channel_id=1, source_target_pairs={{0,16},{16,0},{1,17},{17,1},{2,18},{18,2},{3,19},{19,3},{4,20},{20... | collective-permute-start | bytes 48008 | tf_op jit(solution)/shard_map/ppermute | solution.py:17
  55.4 6.2 %copy-start.27 = (s32[2,3,512]{2,1,0:T(4,128)}, s32[2,3,512]{2,1,0:T(4,128)S(1)}, u32[]{:S(2)}) copy-start(s32[2,3,512]{2,1,0:T(4,128)S(1)} %get-tuple-element.815) | copy-start | bytes 36868 | tf_op jit(solution)/shard_map/while
  55.4 6.2 %copy-start.31 = (s32[2]{0:T(128)}, s32[2]{0:T(128)S(1)}, u32[]{:S(2)}) copy-start(s32[2]{0:T(128)S(1)} %get-tuple-element.814) | copy-start | bytes 28 | tf_op jit(solution)/shard_map/while
  55.4 6.2 %copy-start.36 = (s32[2]{0:T(128)}, s32[2]{0:T(128)S(1)}, u32[]{:S(2)}) copy-start(s32[2]{0:T(128)S(1)} %get-tuple-element.817) | copy-start | bytes 28 | tf_op jit(solution)/shard_map/while
  55.4 6.2 %copy-start.38 = (s32[2]{0:T(128)}, s32[2]{0:T(128)S(1)}, u32[]{:S(2)}) copy-start(s32[2]{0:T(128)S(1)} %get-tuple-element.816) | copy-start | bytes 28 | tf_op jit(solution)/shard_map/while
  55.4 6.2 %copy-start.40 = (s32[2]{0:T(128)}, s32[2]{0:T(128)S(1)}, u32[]{:S(2)}) copy-start(s32[2]{0:T(128)S(1)} %get-tuple-element.820) | copy-start | bytes 28 | tf_op jit(solution)/shard_map/while
  55.4 8.9 %copy-start.25 = (s32[2,4,1000]{2,1,0:T(4,128)}, s32[2,4,1000]{2,1,0:T(4,128)S(1)}, u32[]{:S(2)}) copy-start(s32[2,4,1000]{2,1,0:T(4,128)S(1)} %get-tuple-element.821) | copy-start | bytes 96004 | tf_op jit(solution)/shard_map/while
  61.8 5.2 copy-start.5
  88.7 6.9 %copy-start.26 = (s32[2,4,1000]{2,1,0:T(4,128)S(1)}, s32[2,4,1000]{2,1,0:T(4,128)}, u32[]{:S(2)}) copy-start(s32[2,4,1000]{2,1,0:T(4,128)} %copy-done.25) | copy-start | bytes 96004 | tf_op jit(solution)/shard_map/while
  88.7 6.9 %copy-start.28 = (s32[2,3,512]{2,1,0:T(4,128)S(1)}, s32[2,3,512]{2,1,0:T(4,128)}, u32[]{:S(2)}) copy-start(s32[2,3,512]{2,1,0:T(4,128)} %copy-done.27) | copy-start | bytes 36868 | tf_op jit(solution)/shard_map/while
  88.8 6.9 %copy-start.32 = (s32[2]{0:T(128)S(1)}, s32[2]{0:T(128)}, u32[]{:S(2)}) copy-start(s32[2]{0:T(128)} %copy-done.31) | copy-start | bytes 28 | tf_op jit(solution)/shard_map/while
  88.8 6.9 %copy-start.37 = (s32[2]{0:T(128)S(1)}, s32[2]{0:T(128)}, u32[]{:S(2)}) copy-start(s32[2]{0:T(128)} %copy-done.36) | copy-start | bytes 28 | tf_op jit(solution)/shard_map/while
  88.8 6.9 %copy-start.39 = (s32[2]{0:T(128)S(1)}, s32[2]{0:T(128)}, u32[]{:S(2)}) copy-start(s32[2]{0:T(128)} %copy-done.38) | copy-start | bytes 28 | tf_op jit(solution)/shard_map/while
  88.8 6.9 %copy-start.41 = (s32[2]{0:T(128)S(1)}, s32[2]{0:T(128)}, u32[]{:S(2)}) copy-start(s32[2]{0:T(128)} %copy-done.40) | copy-start | bytes 28 | tf_op jit(solution)/shard_map/while
  95.7 6.2 %copy-start.27 = (s32[2,3,512]{2,1,0:T(4,128)}, s32[2,3,512]{2,1,0:T(4,128)S(1)}, u32[]{:S(2)}) copy-start(s32[2,3,512]{2,1,0:T(4,128)S(1)} %get-tuple-element.815) | copy-start | bytes 36868 | tf_op jit(solution)/shard_map/while
  95.7 6.2 %copy-start.31 = (s32[2]{0:T(128)}, s32[2]{0:T(128)S(1)}, u32[]{:S(2)}) copy-start(s32[2]{0:T(128)S(1)} %get-tuple-element.814) | copy-start | bytes 28 | tf_op jit(solution)/shard_map/while
  95.7 6.2 %copy-start.36 = (s32[2]{0:T(128)}, s32[2]{0:T(128)S(1)}, u32[]{:S(2)}) copy-start(s32[2]{0:T(128)S(1)} %get-tuple-element.817) | copy-start | bytes 28 | tf_op jit(solution)/shard_map/while
  95.7 6.2 %copy-start.38 = (s32[2]{0:T(128)}, s32[2]{0:T(128)S(1)}, u32[]{:S(2)}) copy-start(s32[2]{0:T(128)S(1)} %get-tuple-element.816) | copy-start | bytes 28 | tf_op jit(solution)/shard_map/while
  95.7 6.2 %copy-start.40 = (s32[2]{0:T(128)}, s32[2]{0:T(128)S(1)}, u32[]{:S(2)}) copy-start(s32[2]{0:T(128)S(1)} %get-tuple-element.820) | copy-start | bytes 28 | tf_op jit(solution)/shard_map/while
  95.7 8.9 %copy-start.25 = (s32[2,4,1000]{2,1,0:T(4,128)}, s32[2,4,1000]{2,1,0:T(4,128)S(1)}, u32[]{:S(2)}) copy-start(s32[2,4,1000]{2,1,0:T(4,128)S(1)} %get-tuple-element.821) | copy-start | bytes 96004 | tf_op jit(solution)/shard_map/while
  102.2 5.2 copy-start.5
  129.1 6.9 %copy-start.26 = (s32[2,4,1000]{2,1,0:T(4,128)S(1)}, s32[2,4,1000]{2,1,0:T(4,128)}, u32[]{:S(2)}) copy-start(s32[2,4,1000]{2,1,0:T(4,128)} %copy-done.25) | copy-start | bytes 96004 | tf_op jit(solution)/shard_map/while
  129.1 6.9 %copy-start.28 = (s32[2,3,512]{2,1,0:T(4,128)S(1)}, s32[2,3,512]{2,1,0:T(4,128)}, u32[]{:S(2)}) copy-start(s32[2,3,512]{2,1,0:T(4,128)} %copy-done.27) | copy-start | bytes 36868 | tf_op jit(solution)/shard_map/while
  129.1 6.9 %copy-start.32 = (s32[2]{0:T(128)S(1)}, s32[2]{0:T(128)}, u32[]{:S(2)}) copy-start(s32[2]{0:T(128)} %copy-done.31) | copy-start | bytes 28 | tf_op jit(solution)/shard_map/while
  129.1 6.9 %copy-start.37 = (s32[2]{0:T(128)S(1)}, s32[2]{0:T(128)}, u32[]{:S(2)}) copy-start(s32[2]{0:T(128)} %copy-done.36) | copy-start | bytes 28 | tf_op jit(solution)/shard_map/while
  129.1 6.9 %copy-start.39 = (s32[2]{0:T(128)S(1)}, s32[2]{0:T(128)}, u32[]{:S(2)}) copy-start(s32[2]{0:T(128)} %copy-done.38) | copy-start | bytes 28 | tf_op jit(solution)/shard_map/while
  129.1 6.9 %copy-start.41 = (s32[2]{0:T(128)S(1)}, s32[2]{0:T(128)}, u32[]{:S(2)}) copy-start(s32[2]{0:T(128)} %copy-done.40) | copy-start | bytes 28 | tf_op jit(solution)/shard_map/while
  137.8 9.4 %copy-start.2 = (f32[1345,200]{1,0:T(8,128)S(1)}, f32[1345,200]{1,0:T(8,128)}, u32[]{:S(2)}) copy-start(f32[1345,200]{1,0:T(8,128)} %get-tuple-element.377) | copy-start | bytes 3228004
  140.0 28.0 %collective-permute-start.4 = (f32[1024,200]{0,1:T(8,128)}, f32[1024,200]{0,1:T(8,128)}, u32[]{:S(2)}, u32[]{:S(2)}) collective-permute-start(f32[1024,200]{0,1:T(8,128)} %slice.233), channel_id=1, source_target_pairs={{0,16},{16,0},{1,17},{17,1},{2,18},{18,2},{3,19},{19,3},{4,20},{20... | collective-permute-start | bytes 2457608 | tf_op jit(solution)/shard_map/ppermute | solution.py:17
  140.0 1.4 collective-permute-start.5
  140.0 5.9 collective-permute-start.6
  140.5 6.1 collective-permute-start.8
  147.2 20.8 %copy-start.17 = (f32[2048,200]{0,1:T(8,128)S(1)}, f32[2048,200]{0,1:T(8,128)}, u32[]{:S(2)}) copy-start(f32[2048,200]{0,1:T(8,128)} %copy.92) | copy-start | bytes 4915204
  148.6 20.6 %copy-start.34 = (f32[1024]{0:T(1024)S(1)}, f32[1024]{0:T(1024)}, u32[]{:S(2)}) copy-start(f32[1024]{0:T(1024)} %param.12) | copy-start | bytes 12292
  148.6 20.7 %copy-start.24 = (f32[1024,200]{0,1:T(8,128)S(1)}, f32[1024,200]{0,1:T(8,128)}, u32[]{:S(2)}) copy-start(f32[1024,200]{0,1:T(8,128)} %param.11) | copy-start | bytes 2457604
  148.6 447.1 %all-reduce.5.cloned.1.call-start = ((), (), s32[]{:S(2)}) async-start(), calls=%async_computation.1 | async-start | bytes 2252800 | tf_op jit(solution)/shard_map/psum | solution.py:172
  169.3 151.1 %copy-start.29 = (f32[1345]{0:T(1024)S(1)}, f32[1345]{0:T(1024)}, u32[]{:S(2)}) copy-start(f32[1345]{0:T(1024)} %param.14) | copy-start | bytes 16144
  171.6 148.9 %copy-start.21 = (f32[1345,200]{0,1:T(8,128)S(1)}, f32[1345,200]{0,1:T(8,128)}, u32[]{:S(2)}) copy-start(f32[1345,200]{0,1:T(8,128)} %param.13) | copy-start | bytes 3228004
  171.6 151.8 %collective-permute-start.7 = (f32[1024,200]{0,1:T(8,128)}, f32[1024,200]{0,1:T(8,128)}, u32[]{:S(2)}, u32[]{:S(2)}) collective-permute-start(f32[1024,200]{0,1:T(8,128)} %divide_subtract_fusion.3), channel_id=1, source_target_pairs={{0,1},{1,0},{2,3},{3,2},{4,5},{5,4},{6,7},{7,6},{8,9},{9,8},{10,11... | collective-permute-start | bytes 2457608 | tf_op jit(solution)/shard_map/ppermute | solution.py:17
  339.2 5.2 copy-start.7
  422.1 175.1 %copy-start.30 = (f32[1345]{0:T(1024)S(1)}, f32[1345]{0:T(1024)}, u32[]{:S(2)}) copy-start(f32[1345]{0:T(1024)} %param.14) | copy-start | bytes 16144
  422.1 175.7 %copy-start.20 = (f32[1345,200]{0,1:T(8,128)S(1)}, f32[1345,200]{0,1:T(8,128)}, u32[]{:S(2)}) copy-start(f32[1345,200]{0,1:T(8,128)} %copy-done.19) | copy-start | bytes 3228004
  423.4 175.5 %collective-permute-start.9 = (f32[1024,200]{0,1:T(8,128)S(1)}, f32[1024,200]{0,1:T(8,128)S(1)}, u32[]{:S(2)}, u32[]{:S(2)}) collective-permute-start(f32[1024,200]{0,1:T(8,128)S(1)} %slice.235), channel_id=1, source_target_pairs={{0,1},{1,0},{2,3},{3,2},{4,5},{5,4},{6,7},{7,6},{8,9},{9,8},{10,11... | collective-permute-start | bytes 2457608 | tf_op jit(solution)/shard_map/ppermute | solution.py:17
  (34 other events, 92.8 us)
Sparse Core Ops, SparseCore 0:
  148.8 170.2 all-reduce.2
  420.5 175.1 all-reduce.4
where the time goes:
time: 614 us; the launch traced here: 610 us
  waiting for transfers between devices  367 us (60%)
  local copies, waits for them, and re-layouts  98.2 us (16%)
  other arithmetic  93.3 us (15%)
  matrix products  21.9 us (4%)
  between operations  16.9 us (3%)
  starting transfers between devices  7.76 us (1%)
    psum x2, waiting for transfers between devices, body(): relation_total = lax.psum(relation_grads, 'dom')  320 us
    ppermute x10, waiting for transfers between devices, swapped(): return lax.ppermute(block, axis, route)  47.2 us
    scatter-add x12, other arithmetic, block_terms(): grad_table = grad_table.at[source].add(source_grad).at[target].add(target...  43.6 us
    gather x4, local copies, waits for them, and re-layouts, block_terms(): neg_rows = table[negative_ids]  20.7 us
    scatter-add x4, other arithmetic, block_terms(): grad_relation = grad_relation.at[relation].add(relation_grad)  15.9 us
    while x8, local copies, waits for them, and re-layouts, bucket_pass(): return lax.fori_loop(first, last, visit, carry)  15.6 us
  transfers between devices with their start and end apart: 12, of which 6 were waited for; matrix products, arithmetic and copies ran while one was open for 5% of the time, Pallas kernels for 0%

commit v1 on v0

v1 whole, which is shorter than its diff:
```python
import jax
import jax.numpy as jnp
from jax import lax
from jax.sharding import PartitionSpec as P

RATE = 0.2
HIGH = lax.Precision.HIGH
F32 = jnp.float32


def swapped(block, axis, apart):
    count = lax.axis_size(axis)
    route = []
    for low in range(count):
        high = low | 1 << apart
        if high != low and high < count:
            route += [(low, high), (high, low)]
    return lax.ppermute(block, axis, route)


def dot(a, b, ca, cb):
    return lax.dot_general(
        a, b, (((ca,), (cb,)), ((), ())), precision=HIGH, preferred_element_type=F32
    )


def adagrad(param, state, grad):
    new_state = state + jnp.mean(grad * grad, axis=1)
    return (param - RATE * grad / jnp.sqrt(new_state)[:, None], new_state)


def body(entities, entity_state, relations, relation_state, edges, negatives, counts):
    rows, dim = entities.shape
    half = dim // 2
    blocks, neg = negatives.shape[1:]
    slots = edges.shape[2]
    block = slots // blocks
    lane = 128
    levels = lax.axis_size("dom").bit_length() - 1
    bits = (levels - 1, 0)
    infos = []
    for r, bit in enumerate(bits):
        packed = jnp.concatenate([edges[r, 2], negatives[r].reshape(-1), counts[r]])
        infos.append(swapped(packed, "dom", bit))
    for r, bit in enumerate(bits):
        src_hot = (edges[r, 0][:, None] == jnp.arange(rows)[None, :]).astype(F32)
        rel_hot = (edges[r, 1][:, None] == jnp.arange(relations.shape[0])[None, :]).astype(F32)
        s = dot(src_hot, entities, 1, 0)
        w = dot(rel_hot, relations, 1, 0)
        s_re, s_im, w_re, w_im = s[:, :half], s[:, half:], w[:, :half], w[:, half:]
        q = jnp.concatenate([s_re * w_re - s_im * w_im, s_re * w_im + s_im * w_re], axis=1)
        q_in = swapped(q, "dom", bit)
        tgt = infos[r][:slots]
        ids = infos[r][slots : slots + blocks * neg].reshape(blocks, neg)
        live = jnp.arange(slots) < infos[r][slots + blocks * neg]
        hi_hot = (ids[:, :, None] // lane == jnp.arange(rows // lane)).astype(jnp.bfloat16)
        lo_hot = (ids[:, :, None] % lane == jnp.arange(lane)).astype(jnp.bfloat16)
        times = lax.dot_general(
            hi_hot, lo_hot, (((1,), (1,)), ((0,), (0,))), preferred_element_type=F32
        ).reshape(blocks, 1, rows) * (1.0 / neg)
        score = dot(q_in, entities, 1, 1)
        small = jnp.exp(-jnp.abs(score))
        large = 1.0 / (1.0 + small)
        small = small * large
        up_sig = jnp.where(score >= 0, large, small)
        down_sig = jnp.where(score >= 0, small, large)
        weight = (up_sig.reshape(blocks, block, rows) * times).reshape(slots, rows)
        weight -= jnp.where(tgt[:, None] == jnp.arange(rows)[None, :], down_sig, 0.0)
        weight = jnp.where(live[:, None], weight, 0.0)
        u = swapped(dot(weight, entities, 1, 0), "dom", bit)
        grad = dot(weight, q_in, 0, 0)
        u_re, u_im = u[:, :half], u[:, half:]
        s_grad = jnp.concatenate([u_re * w_re + u_im * w_im, u_im * w_re - u_re * w_im], axis=1)
        w_grad = jnp.concatenate([u_re * s_re + u_im * s_im, u_im * s_re - u_re * s_im], axis=1)
        h = lax.psum(dot(rel_hot, w_grad, 0, 0), "dom")
        grad += dot(src_hot, s_grad, 0, 0)
        entities, entity_state = adagrad(entities, entity_state, grad)
        relations, relation_state = adagrad(relations, relation_state, h)
    return (entities, entity_state, relations, relation_state)


def solution(mesh):
    return jax.shard_map(
        body,
        mesh=mesh,
        in_specs=(
            P("dom", None),
            P("dom"),
            P(),
            P(),
            P(None, None, "dom"),
            P(None, "dom", None),
            P(None, "dom"),
        ),
        out_specs=(P("dom", None), P("dom"), P(), P()),
        check_vma=False,
    )
```

time: 614 us -> 359 us (0.58)
  local copies, waits for them, and re-layouts: 98.2 us -> 9.29 us
  other arithmetic: 93.3 us -> 12 us
  waiting for transfers between devices: 367 us -> 290 us
    psum x2, waiting for transfers between devices: 320 us -> 252 us  [body(): h = lax.psum(dot(rel_hot, w_grad, 0, 0), 'dom')]
    scatter-add x16 -> x0, other arithmetic: 59.5 us -> none  [the longest x12 43.6 us: block_terms(): grad_table = grad_table.at[source].add(source_grad).at[target].add(target...]
    gather x20 -> x0, local copies, waits for them, and re-layouts: 48.3 us -> none  [the longest x4 20.7 us: block_terms(): neg_rows = table[negative_ids]]
    while x136 -> x0, local copies, waits for them, and re-layouts: 17.4 us -> none  [the longest x8 15.6 us: bucket_pass(): return lax.fori_loop(first, last, visit, carry)]
    select_n x14 -> x2, other arithmetic: 13.7 us -> 0.07 us  [body(): ids[:, :, None] // lane == jnp.arange(rows // lane)]
    dynamic_slice x16 -> x0, local copies, waits for them, and re-layouts: 12.6 us -> none  [the longest x4 3.72 us: visit(): target_shift[which]]
    ppermute x10 -> x6, waiting for transfers between devices: 47.2 us -> 38 us  [swapped(): return lax.ppermute(block, axis, route)]
    dot_general x12 -> x16, matrix products: 21.9 us -> 27.6 us  [the longest x14 25 us: dot(): lax.dot_general(a, b, (((ca,), (cb,)), ((), ())), precision=HIGH, preferr...]
  transfers between devices with their start and end apart: 12 -> 8, of which waited for: 6 -> 6; matrix products, arithmetic and copies ran while one was open for 5% -> 5% of each run, Pallas kernels for 0% -> 0%
where the time goes in v1:
time: 359 us; the launch traced here: 358 us
  waiting for transfers between devices  290 us (81%)
  matrix products  27.6 us (8%)
  between operations  14.5 us (4%)
  other arithmetic  12 us (3%)
  local copies, waits for them, and re-layouts  9.29 us (3%)
  starting transfers between devices  4.57 us (1%)
    psum x2, waiting for transfers between devices, body(): h = lax.psum(dot(rel_hot, w_grad, 0, 0), 'dom')  252 us
    ppermute x6, waiting for transfers between devices, swapped(): return lax.ppermute(block, axis, route)  38 us
    dot_general x14, matrix products, dot(): lax.dot_general(a, b, (((ca,), (cb,)), ((), ())), precision=HIGH, preferr...  25 us
  transfers between devices with their start and end apart: 8, of which 6 were waited for; matrix products, arithmetic and copies ran while one was open for 5% of the time, Pallas kernels for 0%

profile of v1, /device:TPU:0, one launch (start us, length us, event | category | flops | bytes accessed | tf_op | source)
XLA Modules:
  0.0 358.2 jit_solution(12648334035743052897)
XLA Ops:
  7.2 1.4 fusion.57
  8.7 0.7 fusion.56
  9.5 1.3 fusion.58
  10.8 0.7 concatenate.24
  11.5 4.1 %collective-permute-start = (s32[4513]{0:T(1024)S(1)}, s32[4513]{0:T(1024)S(1)}, u32[]{:S(2)}, u32[]{:S(2)}) collective-permute-start(s32[4513]{0:T(1024)S(1)} %concatenate.24), channel_id=1, source_target_pairs={{0,16},{16,0},{1,17},{17,1},{2,18},{18,2},{3,19},{19,3},{4,20},{20... | collective-permute-start | bytes 54164 | tf_op jit(solution)/shard_map/ppermute | solution.py:18
  15.6 2.6 fusion.3
  18.2 1.0 fusion.15
  19.2 0.8 copy-done.3
  20.3 1.3 fusion.25
  21.6 0.6 slice.112
  22.2 0.6 iota_compare_fusion.31
  22.9 17.9 %collective-permute-done.1 = f32[512,200]{0,1:T(8,128)S(1)} collective-permute-done((f32[512,200]{0,1:T(8,128)S(1)}, f32[512,200]{0,1:T(8,128)S(1)}, u32[]{:S(2)}, u32[]{:S(2)}) %collective-permute-start.1) | collective-permute-done | bytes 409632 | tf_op jit(solution)/shard_map/ppermute | solution.py:18
  40.8 0.7 copy-done.4
  41.5 3.0 fusion.6
  44.5 1.9 fusion.59
  46.5 0.7 concatenate.27
  47.2 1.2 collective-permute-done.3
  48.4 0.7 broadcast_in_dim_reshape.9
  49.1 17.2 %collective-permute-done.2 = f32[512,200]{0,1:T(8,128)S(1)} collective-permute-done((f32[512,200]{0,1:T(8,128)}, f32[512,200]{0,1:T(8,128)S(1)}, u32[]{:S(2)}, u32[]{:S(2)}) %collective-permute-start.2) | collective-permute-done | bytes 409632 | tf_op jit(solution)/shard_map/ppermute | solution.py:18
  66.3 1.9 multiply_add_fusion.3
  68.2 2.1 fusion.2
  70.3 0.2 all-reduce.5.cloned.1.call-start
  70.6 1.8 fusion.14
  72.4 0.9 multiply_reduce_fusion.3
  73.4 0.2 copy-done.1
  73.5 0.1 divide_subtract_fusion.3
  73.7 1.0 fusion.13
  74.7 126.0 %all-reduce.3.cloned.1.call-done = f32[1345,200]{0,1:T(8,128)} async-done(((f32[1345,200]{0,1:T(8,128)}), f32[1345,200]{0,1:T(8,128)}) %all-reduce.3.cloned.1.call-update) | async-done | bytes 1076016 | tf_op jit(solution)/shard_map/psum | solution.py:75
  200.7 1.3 multiply_reduce_fusion.1
  202.1 2.7 fusion.1
  204.8 0.1 multiply_subtract_fusion.2
  205.0 0.5 copy-done.10
  205.5 1.3 fusion.23
  206.8 0.6 slice.121
  207.4 0.6 iota_compare_fusion.30
  208.1 2.0 fusion.10
  210.1 1.2 fusion.60
  211.4 1.7 collective-permute-done.5
  213.1 0.8 multiply_add_fusion
  214.0 2.1 fusion
  216.1 1.8 fusion.12
  217.9 0.9 multiply_reduce_fusion.2
  218.9 0.6 fusion.55
  219.5 1.1 divide_subtract_fusion.2
  220.6 126.3 %all-reduce.5.cloned.1.call-done = f32[1345,200]{0,1:T(8,128)} async-done(((f32[1345,200]{0,1:T(8,128)}), f32[1345,200]{0,1:T(8,128)}) %all-reduce.5.cloned.1.call-update) | async-done | bytes 1076016 | tf_op jit(solution)/shard_map/psum | solution.py:75
  346.9 1.3 multiply_reduce_fusion
  348.2 0.6 fusion.54
  348.8 2.5 divide_subtract_fusion
  (65 shorter events, 0.9 us)
Async XLA Ops:
  7.2 11.0 %copy-start = (f32[1024,200]{0,1:T(8,128)S(1)}, f32[1024,200]{0,1:T(8,128)}, u32[]{:S(2)}) copy-start(f32[1024,200]{0,1:T(8,128)} %param.7) | copy-start | bytes 2457604
  7.2 193.5 %all-reduce.3.cloned.1.call-start = ((), (), s32[]{:S(2)}) async-start(), calls=%async_computation | async-start | bytes 2252800 | tf_op jit(solution)/shard_map/psum | solution.py:75
  8.6 65.0 %copy-start.18 = (s32[1,1,512]{2,0,1:T(1,128)}, s32[1,1,512]{2,0,1:T(1,128)S(1)}, u32[]{:S(2)}) copy-start(s32[1,1,512]{2,0,1:T(1,128)S(1)} %get-tuple-element.35) | copy-start | bytes 6148
  11.5 8.6 %collective-permute-start = (s32[4513]{0:T(1024)S(1)}, s32[4513]{0:T(1024)S(1)}, u32[]{:S(2)}, u32[]{:S(2)}) collective-permute-start(s32[4513]{0:T(1024)S(1)} %concatenate.24), channel_id=1, source_target_pairs={{0,16},{16,0},{1,17},{17,1},{2,18},{18,2},{3,19},{19,3},{4,20},{20... | collective-permute-start | bytes 54164 | tf_op jit(solution)/shard_map/ppermute | solution.py:18
  19.2 0.8 copy-start.3
  20.1 20.7 %collective-permute-start.1 = (f32[512,200]{0,1:T(8,128)S(1)}, f32[512,200]{0,1:T(8,128)S(1)}, u32[]{:S(2)}, u32[]{:S(2)}) collective-permute-start(f32[512,200]{0,1:T(8,128)S(1)} %pad_maximum_fusion), channel_id=1, source_target_pairs={{0,16},{16,0},{1,17},{17,1},{2,18},{18,2},{3,19},{19,3},{4,20},{20... | collective-permute-start | bytes 1228808 | tf_op jit(solution)/shard_map/ppermute | solution.py:18
  40.8 0.8 copy-start.4
  46.5 19.8 %collective-permute-start.2 = (f32[512,200]{0,1:T(8,128)}, f32[512,200]{0,1:T(8,128)S(1)}, u32[]{:S(2)}, u32[]{:S(2)}) collective-permute-start(f32[512,200]{0,1:T(8,128)} %fusion.59), channel_id=1, source_target_pairs={{0,16},{16,0},{1,17},{17,1},{2,18},{18,2},{3,19},{19,3},{4,20},{20... | collective-permute-start | bytes 1228808 | tf_op jit(solution)/shard_map/ppermute | solution.py:18
  47.2 1.2 collective-permute-start.3
  48.4 0.7 copy-start.15
  68.2 4.2 %copy-start.5 = (f32[512,200]{0,1:T(8,128)S(1)}, f32[512,200]{0,1:T(8,128)}, u32[]{:S(2)}) copy-start(f32[512,200]{0,1:T(8,128)} %copy-done.4) | copy-start | bytes 1228804
  70.3 276.5 %all-reduce.5.cloned.1.call-start = ((), (), s32[]{:S(2)}) async-start(), calls=%async_computation.1 | async-start | bytes 2252800 | tf_op jit(solution)/shard_map/psum | solution.py:75
  72.4 1.0 copy-start.17
  72.4 1.2 copy-start.1
  73.5 128.5 %copy-start.13 = (f32[1345]{0:T(1024)S(1)}, f32[1345]{0:T(1024)}, u32[]{:S(2)}) copy-start(f32[1345]{0:T(1024)} %param.10) | copy-start | bytes 16144
  73.5 128.5 %copy-start.8 = (f32[1345,200]{0,1:T(8,128)S(1)}, f32[1345,200]{0,1:T(8,128)}, u32[]{:S(2)}) copy-start(f32[1345,200]{0,1:T(8,128)} %param.9) | copy-start | bytes 3228004
  73.5 128.5 %copy-start.19 = (s32[1,1,512]{2,0,1:T(1,128)S(1)}, s32[1,1,512]{2,0,1:T(1,128)}, u32[]{:S(2)}) copy-start(s32[1,1,512]{2,0,1:T(1,128)} %get-tuple-element.34) | copy-start | bytes 6148
  202.0 2.7 copy-start.11
  204.7 0.7 copy-start.10
  204.7 2.0 copy-start.16
  204.8 3.3 slice-start
  204.9 3.1 collective-permute-start.4
  208.1 3.2 copy-start.6
  210.1 3.9 %copy-start.20 = (s32[1,1,512]{2,0,1:T(1,128)S(1)}, s32[1,1,512]{2,0,1:T(1,128)}, u32[]{:S(2)}) copy-start(s32[1,1,512]{2,0,1:T(1,128)} %get-tuple-element.34) | copy-start | bytes 6148
  211.3 1.8 collective-permute-start.5
  213.9 4.0 %copy-start.7 = (f32[512,200]{0,1:T(8,128)S(1)}, f32[512,200]{0,1:T(8,128)}, u32[]{:S(2)}) copy-start(f32[512,200]{0,1:T(8,128)} %copy-done.6) | copy-start | bytes 1228804
  218.9 129.3 %copy-start.14 = (f32[1345]{0:T(1024)S(1)}, f32[1345]{0:T(1024)}, u32[]{:S(2)}) copy-start(f32[1345]{0:T(1024)} %param.10) | copy-start | bytes 16144
  218.9 129.9 %copy-start.2 = (f32[1345,200]{0,1:T(8,128)S(1)}, f32[1345,200]{0,1:T(8,128)}, u32[]{:S(2)}) copy-start(f32[1345,200]{0,1:T(8,128)} %all-reduce.3.cloned.1.call-done) | copy-start | bytes 3228004
  218.9 129.9 %copy-start.9 = (f32[1345,200]{0,1:T(8,128)S(1)}, f32[1345,200]{0,1:T(8,128)}, u32[]{:S(2)}) copy-start(f32[1345,200]{0,1:T(8,128)} %param.9) | copy-start | bytes 3228004
  218.9 129.9 %copy-start.12 = (f32[1345]{0:T(1024)S(1)}, f32[1345]{0:T(1024)}, u32[]{:S(2)}) copy-start(f32[1345]{0:T(1024)} %copy-done.11) | copy-start | bytes 16144
Sparse Core Ops, SparseCore 0:
  70.4 130.1 all-reduce.2
  216.2 130.5 all-reduce.4

commit v2 on v1

--- a/solution.py
+++ b/solution.py
@@ -1,6 +1,10 @@
+import functools
+
 import jax
 import jax.numpy as jnp
 from jax import lax
+from jax.experimental import pallas as pl
+from jax.experimental.pallas import tpu as pltpu
 from jax.sharding import PartitionSpec as P
 
 RATE = 0.2
@@ -27,6 +31,107 @@
 def adagrad(param, state, grad):
     new_state = state + jnp.mean(grad * grad, axis=1)
     return (param - RATE * grad / jnp.sqrt(new_state)[:, None], new_state)
+
+
+def relation_kernel(levels, dim, table_ref, grad_ref, out_ref, acc, landed, send_sem, recv_sem):
+    me = lax.axis_index("dom")
+    rows = grad_ref.shape[0]
+    core = me % 2
+
+    def side_of(bit):
+        return me // 2**bit % 2
+
+    first = list(range(levels))
+    second = list(range(levels))
+    for low in range(1, levels - 1, 2):
+        second[low], second[low + 1] = second[low + 1], second[low]
+    sides, peers = [], []
+    for a, b in zip(first, second):
+        sides.append((1 - core) * side_of(a) + core * side_of(b))
+        step_a = (1 - 2 * side_of(a)) * 2**a
+        step_b = (1 - 2 * side_of(b)) * 2**b
+        peers.append(me + (1 - core) * step_a + core * step_b)
+
+    barrier = pltpu.get_barrier_semaphore()
+    for peer in peers:
+        pl.semaphore_signal(
+            barrier, inc=1, device_id=(peer,), device_id_type=pl.DeviceIdType.MESH
+        )
+    pl.semaphore_wait(barrier, levels)
+
+    def piece(start, size):
+        return pl.ds(pl.multiple_of(start, 8), size)
+
+    start, size, slot = 0, rows, 0
+    source = grad_ref
+    for step in range(levels):
+        size //= 2
+        keep = start + sides[step] * size
+        give = start + (1 - sides[step]) * size
+        copy = pltpu.make_async_remote_copy(
+            src_ref=source.at[piece(give, size)],
+            dst_ref=landed.at[pl.ds(slot, size)],
+            send_sem=send_sem.at[step],
+            recv_sem=recv_sem.at[step],
+            device_id=(peers[step],),
+            device_id_type=pl.DeviceIdType.MESH,
+        )
+        copy.start()
+        copy.wait()
+        if step + 1 < levels:
+            half = size // 2
+            for flip in (1 - sides[step + 1], sides[step + 1]):
+                acc[piece(keep + flip * half, half), :] = (
+                    source[piece(keep + flip * half, half), :]
+                    + landed[piece(slot + flip * half, half), :]
+                )
+        else:
+            acc[piece(keep, size), :] = (
+                source[piece(keep, size), :] + landed[pl.ds(slot, size), :]
+            )
+        source = acc
+        start = keep
+        slot += size
+
+    grad = acc[piece(start, size), :]
+    old = table_ref[piece(start, size), :]
+    state = old[:, dim : dim + 1] + jnp.sum(grad * grad, axis=1, keepdims=True) * (1.0 / dim)
+    new = old - RATE * grad / jnp.sqrt(state)
+    column = lax.broadcasted_iota(jnp.int32, new.shape, 1)
+    out_ref[piece(start, size), :] = jnp.where(column == dim, state, new)
+
+    for step in reversed(range(levels)):
+        copy = pltpu.make_async_remote_copy(
+            src_ref=out_ref.at[piece(start, size)],
+            dst_ref=out_ref.at[piece(start, size)],
+            send_sem=send_sem.at[levels + step],
+            recv_sem=recv_sem.at[levels + step],
+            device_id=(peers[step],),
+            device_id_type=pl.DeviceIdType.MESH,
+        )
+        copy.start()
+        copy.wait()
+        start = start - sides[step] * size
+        size *= 2
+
+
+def relation_update(table, grad, levels, dim, number):
+    vmem = pl.BlockSpec(memory_space=pltpu.VMEM)
+    return pl.pallas_call(
+        functools.partial(relation_kernel, levels, dim),
+        out_shape=jax.ShapeDtypeStruct(table.shape, F32),
+        in_specs=[vmem, vmem],
+        out_specs=vmem,
+        scratch_shapes=[
+            pltpu.VMEM(table.shape, F32),
+            pltpu.VMEM(table.shape, F32),
+            pltpu.SemaphoreType.DMA((2 * levels,)),
+            pltpu.SemaphoreType.DMA((2 * levels,)),
+        ],
+        compiler_params=pltpu.CompilerParams(
+            collective_id=number, has_side_effects=True, vmem_limit_bytes=32 * 2**20
+        ),
+    )(table, grad)
 
 
 def body(entities, entity_state, relations, relation_state, edges, negatives, counts):
@@ -38,15 +143,27 @@
     lane = 128
     levels = lax.axis_size("dom").bit_length() - 1
     bits = (levels - 1, 0)
+    rel_rows = relations.shape[0]
+    unit = 8 * lax.axis_size("dom")
+    wide = -(-(dim + 1) // lane) * lane
+    more = -rel_rows % unit
+    table = jnp.concatenate(
+        [
+            jnp.pad(relations, ((0, more), (0, 0))),
+            jnp.pad(relation_state, (0, more), constant_values=1.0)[:, None],
+            jnp.zeros((rel_rows + more, wide - dim - 1), F32),
+        ],
+        axis=1,
+    )
     infos = []
     for r, bit in enumerate(bits):
         packed = jnp.concatenate([edges[r, 2], negatives[r].reshape(-1), counts[r]])
         infos.append(swapped(packed, "dom", bit))
     for r, bit in enumerate(bits):
         src_hot = (edges[r, 0][:, None] == jnp.arange(rows)[None, :]).astype(F32)
-        rel_hot = (edges[r, 1][:, None] == jnp.arange(relations.shape[0])[None, :]).astype(F32)
+        rel_hot = (edges[r, 1][:, None] == jnp.arange(table.shape[0])[None, :]).astype(F32)
         s = dot(src_hot, entities, 1, 0)
-        w = dot(rel_hot, relations, 1, 0)
+        w = dot(rel_hot, table, 1, 0)[:, :dim]
         s_re, s_im, w_re, w_im = s[:, :half], s[:, half:], w[:, :half], w[:, half:]
         q = jnp.concatenate([s_re * w_re - s_im * w_im, s_re * w_im + s_im * w_re], axis=1)
         q_in = swapped(q, "dom", bit)
@@ -72,11 +189,11 @@
         u_re, u_im = u[:, :half], u[:, half:]
         s_grad = jnp.concatenate([u_re * w_re + u_im * w_im, u_im * w_re - u_re * w_im], axis=1)
         w_grad = jnp.concatenate([u_re * s_re + u_im * s_im, u_im * s_re - u_re * s_im], axis=1)
-        h = lax.psum(dot(rel_hot, w_grad, 0, 0), "dom")
+        w_grad = jnp.pad(w_grad, ((0, 0), (0, wide - dim)))
+        table = relation_update(table, dot(rel_hot, w_grad, 0, 0), levels, dim, r)
         grad += dot(src_hot, s_grad, 0, 0)
         entities, entity_state = adagrad(entities, entity_state, grad)
-        relations, relation_state = adagrad(relations, relation_state, h)
-    return (entities, entity_state, relations, relation_state)
+    return (entities, entity_state, table[:rel_rows, :dim], table[:rel_rows, dim])
 
 
 def solution(mesh):

time: 359 us -> 180 us (0.50)
  waiting for transfers between devices: 290 us -> 38.3 us
  Pallas kernels: 0 us -> 93.5 us
  between operations: 14.5 us -> 0.97 us
  matrix products: 27.6 us -> 21.1 us
  other arithmetic: 12 us -> 6.77 us
  local copies, waits for them, and re-layouts: 9.29 us -> 14.3 us
    psum x2 -> x0, waiting for transfers between devices: 252 us -> none  [body(): h = lax.psum(dot(rel_hot, w_grad, 0, 0), 'dom')]
    pallas_call x0 -> x2, Pallas kernels: none -> 93.5 us  [relation_update(): pl.pallas_call(functools.partial(relation_kernel, levels, dim), out_shape...]
    dot_general x14, matrix products: 25 us -> 18.2 us  [dot(): lax.dot_general(a, b, (((ca,), (cb,)), ((), ())), precision=HIGH, preferr...]
    unnamed x44 -> x18, local copies, waits for them, and re-layouts: 2.25 us -> 6.25 us
  transfers between devices with their start and end apart: 8 -> 6, of which waited for: 6 -> 4; matrix products, arithmetic and copies ran while one was open for 5% -> 8% of each run, Pallas kernels for 0% -> 0%
where the time goes in v2:
time: 180 us
  Pallas kernels  93.5 us (52%)
  waiting for transfers between devices  38.3 us (21%)
  matrix products  21.1 us (12%)
  local copies, waits for them, and re-layouts  14.3 us (8%)
  other arithmetic  6.77 us (4%)
  starting transfers between devices  4.81 us (3%)
    pallas_call x2, Pallas kernels, relation_update(): pl.pallas_call(functools.partial(relation_kernel, levels, dim), out_shape...  93.5 us
    ppermute x6, waiting for transfers between devices, swapped(): return lax.ppermute(block, axis, route)  38.3 us
    dot_general x14, matrix products, dot(): lax.dot_general(a, b, (((ca,), (cb,)), ((), ())), precision=HIGH, preferr...  18.2 us
    unnamed x18, local copies, waits for them, and re-layouts  6.25 us
    ppermute x6, starting transfers between devices, swapped(): return lax.ppermute(block, axis, route)  4.81 us
  transfers between devices with their start and end apart: 6, of which 4 were waited for; matrix products, arithmetic and copies ran while one was open for 8% of the time, Pallas kernels for 0%

profile of v2, /device:TPU:0, one launch (start us, length us, event | category | flops | bytes accessed | tf_op | source)
XLA Modules:
  0.0 179.8 jit_solution(15420056035002688314)
XLA Ops:
  0.6 1.3 fusion.69
  2.0 0.8 fusion.68
  2.8 0.7 fusion.67
  3.6 0.7 concatenate.27
  4.3 4.1 %collective-permute-start = (s32[4513]{0:T(1024)S(1)}, s32[4513]{0:T(1024)S(1)}, u32[]{:S(2)}, u32[]{:S(2)}) collective-permute-start(s32[4513]{0:T(1024)S(1)} %concatenate.27), channel_id=1, source_target_pairs={{0,16},{16,0},{1,17},{17,1},{2,18},{18,2},{3,19},{19,3},{4,20},{20... | collective-permute-start | bytes 54164 | tf_op jit(solution)/shard_map/ppermute | solution.py:22
  8.4 0.7 pad.16
  9.1 0.3 broadcast_in_dim.27
  9.3 2.8 %copy.13 = f32[1345,200]{1,0:T(8,128)} copy(f32[1345,200]{0,1:T(8,128)} %param.9) | data formatting | bytes 2152000 | tf_op args[2]
  12.2 1.0 fusion.15
  13.2 1.8 fusion.22.table_ref
  15.0 1.3 fusion.3
  16.4 0.1 multiply_subtract_fusion.5
  16.5 0.7 copy-done.5
  17.4 1.5 fusion.30
  18.9 0.6 slice.126
  19.5 0.6 iota_compare_fusion.33
  20.1 17.7 %collective-permute-done.1 = f32[512,200]{0,1:T(8,128)S(1)} collective-permute-done((f32[512,200]{0,1:T(8,128)S(1)}, f32[512,200]{0,1:T(8,128)S(1)}, u32[]{:S(2)}, u32[]{:S(2)}) %collective-permute-start.1) | collective-permute-done | bytes 409632 | tf_op jit(solution)/shard_map/ppermute | solution.py:22
  37.8 2.0 %fusion.6 = f32[512,1024]{1,0:T(8,128)S(1)} fusion(s32[512]{0:T(512)S(1)} %slice.132, f32[4,1024]{1,0:T(4,128)S(1)} %bitcast.40, pred[512]{0:T(512)(128)(4,1)S(1)} %iota_compare_fusion.33, f32[512,200]{0,1:T(8,128)S(1)} %collective-permute-done.1, f32[1024,200]{0,1:T(8,128)S(1)} %copy-done.2), kind=kOutput, calls=%fused_computation.12 | convolution fusion | flops 635961344 | bytes 3344896 | tf_op jit(solution)/shard_map/dot_general | solution.py:26
  39.9 1.3 copy-done
  41.2 1.9 %fusion.70 = f32[512,200]{0,1:T(8,128)} fusion(f32[512,1024]{1,0:T(8,128)S(1)} %fusion.6, f32[1024,200]{0,1:T(8,128)S(1)} %copy-done.2), kind=kOutput, calls=%fused_computation.128 | convolution fusion | flops 629145600 | bytes 3325952 | tf_op jit(solution)/shard_map/dot_general | solution.py:26
  43.2 0.7 concatenate.31
  43.9 1.2 collective-permute-done.3
  45.2 17.8 %collective-permute-done.2 = f32[512,200]{0,1:T(8,128)} collective-permute-done((f32[512,200]{0,1:T(8,128)}, f32[512,200]{0,1:T(8,128)}, u32[]{:S(2)}, u32[]{:S(2)}) %collective-permute-start.2) | collective-permute-done | bytes 409632 | tf_op jit(solution)/shard_map/ppermute | solution.py:22
  63.0 1.4 multiply_add_fusion.3
  64.5 1.4 fusion.18.grad_ref
  65.9 44.7 %shard_map.102.table_ref = f32[1536,256]{1,0:T(8,128)S(1)} custom-call(f32[1536,256]{1,0:T(8,128)S(1)} %fusion.22.table_ref, f32[1536,256]{1,0:T(8,128)S(1)} %fusion.18.grad_ref), custom_call_target="tpu_custom_call" | custom-call | tf_op jit(solution)/shard_map/pallas_call | solution.py:120
  110.7 0.9 fusion.14
  111.6 0.9 multiply_reduce_fusion.1
  112.5 0.2 divide_subtract_fusion.1
  112.7 1.0 fusion.13
  113.7 1.3 fusion.1
  115.2 0.4 collective-permute-start.4
  115.7 1.4 fusion.28
  117.1 0.6 slice.135
  117.7 0.6 iota_compare_fusion.32
  118.4 2.0 %fusion.10 = f32[512,1024]{1,0:T(8,128)S(1)} fusion(s32[512]{0:T(512)S(1)} %slice.141, f32[4,1024]{1,0:T(4,128)S(1)} %bitcast.41, pred[512]{0:T(512)(128)(4,1)S(1)} %iota_compare_fusion.32, f32[512,200]{0,1:T(8,128)S(1)} %collective-permute-done.4, f32[1024,200]{0,1:T(8,128)S(1)} %divide_subtract_fusion.1), kind=kOutput, calls=%fused_computation.16 | convolution fusion | flops 635961344 | bytes 3344896 | tf_op jit(solution)/shard_map/dot_general | solution.py:26
  120.3 1.2 fusion.71
  121.5 0.2 collective-permute-start.5
  121.7 1.6 collective-permute-done.5
  123.3 0.2 multiply_add_fusion
  123.5 1.4 fusion.20.grad_ref
  125.0 48.8 %shard_map.103 = f32[1536,256]{1,0:T(8,128)S(1)} custom-call(f32[1536,256]{1,0:T(8,128)S(1)} %shard_map.102.table_ref, f32[1536,256]{1,0:T(8,128)S(1)} %fusion.20.grad_ref), custom_call_target="tpu_custom_call" | custom-call | tf_op jit(solution)/shard_map/pallas_call | solution.py:120
  173.7 1.1 slice_reduce_fusion
  174.9 0.9 fusion.12
  175.8 0.9 multiply_reduce_fusion
  176.7 0.6 fusion.66
  177.3 1.4 copy.15
  178.7 1.0 divide_subtract_fusion
  (36 shorter events, 0.9 us)
Async XLA Ops:
  0.6 11.6 %copy-start.2 = (f32[1024,200]{0,1:T(8,128)S(1)}, f32[1024,200]{0,1:T(8,128)}, u32[]{:S(2)}) copy-start(f32[1024,200]{0,1:T(8,128)} %param.7) | copy-start | bytes 2457604
  4.3 13.0 %collective-permute-start = (s32[4513]{0:T(1024)S(1)}, s32[4513]{0:T(1024)S(1)}, u32[]{:S(2)}, u32[]{:S(2)}) collective-permute-start(s32[4513]{0:T(1024)S(1)} %concatenate.27), channel_id=1, source_target_pairs={{0,16},{16,0},{1,17},{17,1},{2,18},{18,2},{3,19},{19,3},{4,20},{20... | collective-permute-start | bytes 54164 | tf_op jit(solution)/shard_map/ppermute | solution.py:22
  13.2 3.1 %copy-start.3 = (f32[512,200]{0,1:T(8,128)}, f32[512,200]{0,1:T(8,128)S(1)}, u32[]{:S(2)}) copy-start(f32[512,200]{0,1:T(8,128)S(1)} %fusion.15) | copy-start | bytes 1228804
  16.4 0.8 copy-start.5
  17.2 20.7 %collective-permute-start.1 = (f32[512,200]{0,1:T(8,128)S(1)}, f32[512,200]{0,1:T(8,128)S(1)}, u32[]{:S(2)}, u32[]{:S(2)}) collective-permute-start(f32[512,200]{0,1:T(8,128)S(1)} %pad_maximum_fusion), channel_id=1, source_target_pairs={{0,16},{16,0},{1,17},{17,1},{2,18},{18,2},{3,19},{19,3},{4,20},{20... | collective-permute-start | bytes 1228808 | tf_op jit(solution)/shard_map/ppermute | solution.py:22
  39.8 1.3 copy-start
  41.2 21.9 %copy-start.4 = (f32[512,200]{0,1:T(8,128)S(1)}, f32[512,200]{0,1:T(8,128)}, u32[]{:S(2)}) copy-start(f32[512,200]{0,1:T(8,128)} %copy-done.3) | copy-start | bytes 1228804
  43.1 19.9 %collective-permute-start.2 = (f32[512,200]{0,1:T(8,128)}, f32[512,200]{0,1:T(8,128)}, u32[]{:S(2)}, u32[]{:S(2)}) collective-permute-start(f32[512,200]{0,1:T(8,128)} %fusion.70), channel_id=1, source_target_pairs={{0,16},{16,0},{1,17},{17,1},{2,18},{18,2},{3,19},{19,3},{4,20},{20... | collective-permute-start | bytes 1228808 | tf_op jit(solution)/shard_map/ppermute | solution.py:22
  43.9 1.2 collective-permute-start.3
  65.9 45.6 %copy-start.1 = (f32[512,1024]{1,0:T(8,128)S(1)}, f32[512,1024]{1,0:T(8,128)}, u32[]{:S(2)}) copy-start(f32[512,1024]{1,0:T(8,128)} %copy-done) | copy-start | bytes 6291460
  111.6 0.9 copy-start.6
  115.2 3.2 %collective-permute-start.4 = (f32[512,200]{0,1:T(8,128)S(1)}, f32[512,200]{0,1:T(8,128)S(1)}, u32[]{:S(2)}, u32[]{:S(2)}) collective-permute-start(f32[512,200]{0,1:T(8,128)S(1)} %pad_maximum_fusion.1), channel_id=1, source_target_pairs={{0,1},{1,0},{2,3},{3,2},{4,5},{5,4},{6,7},{7,6},{8,9},{9,8},{10,11... | collective-permute-start | bytes 1228808 | tf_op jit(solution)/shard_map/ppermute | solution.py:22
  121.5 1.8 %collective-permute-start.5 = (f32[512,200]{0,1:T(8,128)S(1)}, f32[512,200]{0,1:T(8,128)S(1)}, u32[]{:S(2)}, u32[]{:S(2)}) collective-permute-start(f32[512,200]{0,1:T(8,128)S(1)} %fusion.71), channel_id=1, source_target_pairs={{0,1},{1,0},{2,3},{3,2},{4,5},{5,4},{6,7},{7,6},{8,9},{9,8},{10,11... | collective-permute-start | bytes 1228808 | tf_op jit(solution)/shard_map/ppermute | solution.py:22

commit v3 on v1

--- a/solution.py
+++ b/solution.py
@@ -1,6 +1,10 @@
+import functools
+
 import jax
 import jax.numpy as jnp
 from jax import lax
+from jax.experimental import pallas as pl
+from jax.experimental.pallas import tpu as pltpu
 from jax.sharding import PartitionSpec as P
 
 RATE = 0.2
@@ -27,6 +31,112 @@
 def adagrad(param, state, grad):
     new_state = state + jnp.mean(grad * grad, axis=1)
     return (param - RATE * grad / jnp.sqrt(new_state)[:, None], new_state)
+
+
+def relation_kernel(levels, dim, table_ref, grad_ref, out_ref, acc, landed, send_sem, recv_sem):
+    me = lax.axis_index("dom")
+    rows = grad_ref.shape[0]
+    streams = 3 if rows % (24 * 2**levels) == 0 else 1
+    sides = [me // 2**bit % 2 for bit in range(levels)]
+    peers = [me + (1 - 2 * sides[bit]) * 2**bit for bit in range(levels)]
+    inner = list(range(1, levels - 1))
+    orders = []
+    for stream in range(streams):
+        turn = stream % max(len(inner), 1)
+        orders.append([0] + inner[turn:] + inner[:turn] + [levels - 1])
+
+    barrier = pltpu.get_barrier_semaphore()
+    for peer in peers:
+        pl.semaphore_signal(
+            barrier, inc=1, device_id=(peer,), device_id_type=pl.DeviceIdType.MESH
+        )
+    pl.semaphore_wait(barrier, levels)
+
+    def piece(start, size):
+        return pl.ds(pl.multiple_of(start, 8), size)
+
+    def send(source, target, stream, step, phase, bit):
+        number = (phase * streams + stream) * levels + step
+        copy = pltpu.make_async_remote_copy(
+            src_ref=source,
+            dst_ref=target,
+            send_sem=send_sem.at[number],
+            recv_sem=recv_sem.at[number],
+            device_id=(peers[bit],),
+            device_id_type=pl.DeviceIdType.MESH,
+        )
+        copy.start()
+        return copy
+
+    size = rows // streams
+    starts = [stream * size for stream in range(streams)]
+    slots = [stream * size for stream in range(streams)]
+    source = grad_ref
+    for step in range(levels):
+        size //= 2
+        copies = []
+        for stream in range(streams):
+            side = sides[orders[stream][step]]
+            give = starts[stream] + (1 - side) * size
+            copies.append(
+                send(
+                    source.at[piece(give, size)],
+                    landed.at[pl.ds(slots[stream], size)],
+                    stream,
+                    step,
+                    0,
+                    orders[stream][step],
+                )
+            )
+        for stream in range(streams):
+            keep = starts[stream] + sides[orders[stream][step]] * size
+            copies[stream].wait()
+            acc[piece(keep, size), :] = (
+                source[piece(keep, size), :] + landed[pl.ds(slots[stream], size), :]
+            )
+            starts[stream] = keep
+            slots[stream] += size
+        source = acc
+
+    for stream in range(streams):
+        own = piece(starts[stream], size)
+        grad = acc[own, :]
+        old = table_ref[own, :]
+        state = old[:, dim : dim + 1] + jnp.sum(grad * grad, axis=1, keepdims=True) * (1.0 / dim)
+        new = old - RATE * grad / jnp.sqrt(state)
+        column = lax.broadcasted_iota(jnp.int32, new.shape, 1)
+        out_ref[own, :] = jnp.where(column == dim, state, new)
+
+    for step in reversed(range(levels)):
+        copies = []
+        for stream in range(streams):
+            own = piece(starts[stream], size)
+            copies.append(
+                send(out_ref.at[own], out_ref.at[own], stream, step, 1, orders[stream][step])
+            )
+        for stream in range(streams):
+            copies[stream].wait()
+            starts[stream] = starts[stream] - sides[orders[stream][step]] * size
+        size *= 2
+
+
+def relation_update(table, grad, levels, dim, number):
+    vmem = pl.BlockSpec(memory_space=pltpu.VMEM)
+    return pl.pallas_call(
+        functools.partial(relation_kernel, levels, dim),
+        out_shape=jax.ShapeDtypeStruct(table.shape, F32),
+        in_specs=[vmem, vmem],
+        out_specs=vmem,
+        scratch_shapes=[
+            pltpu.VMEM(table.shape, F32),
+            pltpu.VMEM(table.shape, F32),
+            pltpu.SemaphoreType.DMA((6 * levels,)),
+            pltpu.SemaphoreType.DMA((6 * levels,)),
+        ],
+        compiler_params=pltpu.CompilerParams(
+            collective_id=number, has_side_effects=True, vmem_limit_bytes=32 * 2**20
+        ),
+    )(table, grad)
 
 
 def body(entities, entity_state, relations, relation_state, edges, negatives, counts):
@@ -38,17 +148,29 @@
     lane = 128
     levels = lax.axis_size("dom").bit_length() - 1
     bits = (levels - 1, 0)
+    rel_rows = relations.shape[0]
+    unit = 8 * lax.axis_size("dom")
+    wide = -(-(dim + 1) // lane) * lane
+    more = -rel_rows % unit
+    table = jnp.concatenate(
+        [
+            jnp.pad(relations, ((0, more), (0, 0))),
+            jnp.pad(relation_state, (0, more), constant_values=1.0)[:, None],
+            jnp.zeros((rel_rows + more, wide - dim - 1), F32),
+        ],
+        axis=1,
+    )
     infos = []
     for r, bit in enumerate(bits):
         packed = jnp.concatenate([edges[r, 2], negatives[r].reshape(-1), counts[r]])
         infos.append(swapped(packed, "dom", bit))
     for r, bit in enumerate(bits):
         src_hot = (edges[r, 0][:, None] == jnp.arange(rows)[None, :]).astype(F32)
-        rel_hot = (edges[r, 1][:, None] == jnp.arange(relations.shape[0])[None, :]).astype(F32)
-        s = dot(src_hot, entities, 1, 0)
-        w = dot(rel_hot, relations, 1, 0)
-        s_re, s_im, w_re, w_im = s[:, :half], s[:, half:], w[:, :half], w[:, half:]
-        q = jnp.concatenate([s_re * w_re - s_im * w_im, s_re * w_im + s_im * w_re], axis=1)
+        rel_hot = (edges[r, 1][:, None] == jnp.arange(table.shape[0])[None, :]).astype(F32)
+        s = dot(entities, src_hot, 0, 1)
+        w = dot(table, rel_hot, 0, 1)[:dim]
+        s_re, s_im, w_re, w_im = s[:half], s[half:], w[:half], w[half:]
+        q = jnp.concatenate([s_re * w_re - s_im * w_im, s_re * w_im + s_im * w_re], axis=0)
         q_in = swapped(q, "dom", bit)
         tgt = infos[r][:slots]
         ids = infos[r][slots : slots + blocks * neg].reshape(blocks, neg)
@@ -58,7 +180,7 @@
         times = lax.dot_general(
             hi_hot, lo_hot, (((1,), (1,)), ((0,), (0,))), preferred_element_type=F32
         ).reshape(blocks, 1, rows) * (1.0 / neg)
-        score = dot(q_in, entities, 1, 1)
+        score = dot(q_in, entities, 0, 1)
         small = jnp.exp(-jnp.abs(score))
         large = 1.0 / (1.0 + small)
         small = small * large
@@ -67,16 +189,16 @@
         weight = (up_sig.reshape(blocks, block, rows) * times).reshape(slots, rows)
         weight -= jnp.where(tgt[:, None] == jnp.arange(rows)[None, :], down_sig, 0.0)
         weight = jnp.where(live[:, None], weight, 0.0)
-        u = swapped(dot(weight, entities, 1, 0), "dom", bit)
-        grad = dot(weight, q_in, 0, 0)
-        u_re, u_im = u[:, :half], u[:, half:]
-        s_grad = jnp.concatenate([u_re * w_re + u_im * w_im, u_im * w_re - u_re * w_im], axis=1)
-        w_grad = jnp.concatenate([u_re * s_re + u_im * s_im, u_im * s_re - u_re * s_im], axis=1)
-        h = lax.psum(dot(rel_hot, w_grad, 0, 0), "dom")
-        grad += dot(src_hot, s_grad, 0, 0)
+        u = swapped(dot(entities, weight, 0, 1), "dom", bit)
+        grad = dot(weight, q_in, 0, 1)
+        u_re, u_im = u[:half], u[half:]
+        s_grad = jnp.concatenate([u_re * w_re + u_im * w_im, u_im * w_re - u_re * w_im], axis=0)
+        w_grad = jnp.concatenate([u_re * s_re + u_im * s_im, u_im * s_re - u_re * s_im], axis=0)
+        w_grad = jnp.pad(w_grad, ((0, wide - dim), (0, 0)))
+        table = relation_update(table, dot(rel_hot, w_grad, 0, 1), levels, dim, r)
+        grad += dot(src_hot, s_grad, 0, 1)
         entities, entity_state = adagrad(entities, entity_state, grad)
-        relations, relation_state = adagrad(relations, relation_state, h)
-    return (entities, entity_state, relations, relation_state)
+    return (entities, entity_state, table[:rel_rows, :dim], table[:rel_rows, dim])
 
 
 def solution(mesh):

time: 359 us -> 161 us (0.45)
  waiting for transfers between devices: 290 us -> 38.3 us
  Pallas kernels: 0 us -> 72.6 us
  between operations: 14.5 us -> 0.97 us
  matrix products: 27.6 us -> 22.3 us
  other arithmetic: 12 us -> 6.77 us
  local copies, waits for them, and re-layouts: 9.29 us -> 14.3 us
    psum x2 -> x0, waiting for transfers between devices: 252 us -> none  [body(): h = lax.psum(dot(rel_hot, w_grad, 0, 0), 'dom')]
    pallas_call x0 -> x2, Pallas kernels: none -> 72.6 us  [relation_update(): pl.pallas_call(functools.partial(relation_kernel, levels, dim), out_shape...]
    dot_general x14, matrix products: 25 us -> 19.4 us  [dot(): lax.dot_general(a, b, (((ca,), (cb,)), ((), ())), precision=HIGH, preferr...]
    unnamed x44 -> x18, local copies, waits for them, and re-layouts: 2.25 us -> 6.25 us
  transfers between devices with their start and end apart: 8 -> 6, of which waited for: 6 -> 4; matrix products, arithmetic and copies ran while one was open for 5% -> 9% of each run, Pallas kernels for 0% -> 0%
where the time goes in v3:
time: 161 us; the launch traced here: 160 us
  Pallas kernels  72.6 us (45%)
  waiting for transfers between devices  38.3 us (24%)
  matrix products  22.3 us (14%)
  local copies, waits for them, and re-layouts  14.3 us (9%)
  other arithmetic  6.77 us (4%)
  starting transfers between devices  4.8 us (3%)
    pallas_call x2, Pallas kernels, relation_update(): pl.pallas_call(functools.partial(relation_kernel, levels, dim), out_shape...  72.6 us
    ppermute x6, waiting for transfers between devices, swapped(): return lax.ppermute(block, axis, route)  38.3 us
    dot_general x14, matrix products, dot(): lax.dot_general(a, b, (((ca,), (cb,)), ((), ())), precision=HIGH, preferr...  19.4 us
    unnamed x18, local copies, waits for them, and re-layouts  6.25 us
    ppermute x6, starting transfers between devices, swapped(): return lax.ppermute(block, axis, route)  4.8 us
  transfers between devices with their start and end apart: 6, of which 4 were waited for; matrix products, arithmetic and copies ran while one was open for 9% of the time, Pallas kernels for 0%

profile of v3, /device:TPU:0, one launch (start us, length us, event | category | flops | bytes accessed | tf_op | source)
XLA Modules:
  0.0 160.0 jit_solution(13174614273365722152)
XLA Ops:
  0.6 1.3 fusion.70
  2.0 0.8 fusion.69
  2.8 0.7 fusion.68
  3.6 0.7 concatenate.27
  4.3 4.1 %collective-permute-start = (s32[4513]{0:T(1024)S(1)}, s32[4513]{0:T(1024)S(1)}, u32[]{:S(2)}, u32[]{:S(2)}) collective-permute-start(s32[4513]{0:T(1024)S(1)} %concatenate.27), channel_id=1, source_target_pairs={{0,16},{16,0},{1,17},{17,1},{2,18},{18,2},{3,19},{19,3},{4,20},{20... | collective-permute-start | bytes 54164 | tf_op jit(solution)/shard_map/ppermute | solution.py:22
  8.4 0.7 pad.16
  9.1 0.3 broadcast_in_dim.27
  9.3 2.8 %copy.13 = f32[1345,200]{1,0:T(8,128)} copy(f32[1345,200]{0,1:T(8,128)} %param.9) | data formatting | bytes 2152000 | tf_op args[2]
  12.2 1.0 fusion.27
  13.2 1.8 %fusion.22.table_ref = f32[1536,256]{1,0:T(8,128)S(1)} fusion(f32[1345,200]{1,0:T(8,128)} %copy.13, f32[1536,1]{1,0:T(8,128)S(1)} %broadcast_in_dim.27, f32[256]{0:T(256)S(1)} %pad.33.clone), kind=kLoop, calls=%fused_computation.33 | loop fusion | flops 1572864 | bytes 2656032 | tf_op jit(solution)/shard_map/concatenate | solution.py:155
  15.0 1.9 %fusion.3 = f32[256,512]{1,0:T(8,128)S(1)} fusion(f32[1536,256]{1,0:T(8,128)S(1)} %fusion.22.table_ref, s32[512]{0:T(512)S(1)} %bitcast.54), kind=kOutput, calls=%fused_computation.5 | convolution fusion | flops 1208745984 | bytes 2099200 | tf_op jit(solution)/shard_map/dot_general | solution.py:26
  17.1 0.7 copy-done.5
  18.0 1.5 fusion.31
  19.5 0.6 slice.126
  20.1 0.6 iota_compare_fusion.35
  20.7 17.7 %collective-permute-done.1 = f32[200,512]{1,0:T(8,128)S(1)} collective-permute-done((f32[200,512]{1,0:T(8,128)S(1)}, f32[200,512]{1,0:T(8,128)S(1)}, u32[]{:S(2)}, u32[]{:S(2)}) %collective-permute-start.1) | collective-permute-done | bytes 409632 | tf_op jit(solution)/shard_map/ppermute | solution.py:22
  38.5 2.0 %fusion.6 = f32[512,1024]{1,0:T(8,128)S(1)} fusion(s32[512]{0:T(512)S(1)} %slice.132, f32[4,1024]{1,0:T(4,128)S(1)} %bitcast.44, pred[512]{0:T(512)(128)(4,1)S(1)} %iota_compare_fusion.35, f32[200,512]{1,0:T(8,128)S(1)} %collective-permute-done.1, f32[1024,200]{0,1:T(8,128)S(1)} %copy-done.2), kind=kOutput, calls=%fused_computation.12 | convolution fusion | flops 635961344 | bytes 3344896 | tf_op jit(solution)/shard_map/dot_general | solution.py:26
  40.5 1.3 copy-done
  41.8 1.9 %convolution_bitcast_fusion = f32[200,512]{1,0:T(8,128)} fusion(f32[512,1024]{1,0:T(8,128)S(1)} %fusion.6, f32[1024,200]{0,1:T(8,128)S(1)} %copy-done.2), kind=kOutput, calls=%fused_computation.42 | convolution fusion | flops 629145600 | bytes 3325952 | tf_op jit(solution)/shard_map/dot_general | solution.py:26
  43.8 0.7 concatenate.31
  44.5 1.2 collective-permute-done.3
  45.8 17.8 %collective-permute-done.2 = f32[200,512]{1,0:T(8,128)} collective-permute-done((f32[200,512]{1,0:T(8,128)}, f32[200,512]{1,0:T(8,128)}, u32[]{:S(2)}, u32[]{:S(2)}) %collective-permute-start.2) | collective-permute-done | bytes 409632 | tf_op jit(solution)/shard_map/ppermute | solution.py:22
  63.6 1.4 multiply_add_fusion.3
  65.1 1.4 fusion.18.grad_ref
  66.5 35.7 %shard_map.102.table_ref = f32[1536,256]{1,0:T(8,128)S(1)} custom-call(f32[1536,256]{1,0:T(8,128)S(1)} %fusion.22.table_ref, f32[1536,256]{1,0:T(8,128)S(1)} %fusion.18.grad_ref), custom_call_target="tpu_custom_call" | custom-call | tf_op jit(solution)/shard_map/pallas_call | solution.py:125
  102.3 0.9 fusion.14
  103.2 0.9 multiply_reduce_fusion.1
  104.1 0.2 divide_subtract_fusion.1
  104.3 1.0 fusion.13
  105.3 1.9 %fusion.1 = f32[256,512]{1,0:T(8,128)S(1)} fusion(f32[1536,256]{1,0:T(8,128)S(1)} %shard_map.102.table_ref, s32[512]{0:T(512)S(1)} %bitcast.50), kind=kOutput, calls=%fused_computation.2 | convolution fusion | flops 1208745984 | bytes 2099200 | tf_op jit(solution)/shard_map/dot_general | solution.py:26
  107.2 0.1 multiply_subtract_fusion.2
  107.4 0.4 collective-permute-start.4
  107.8 1.4 fusion.29
  109.3 0.6 slice.135
  109.9 0.6 iota_compare_fusion.34
  110.5 2.0 %fusion.10 = f32[512,1024]{1,0:T(8,128)S(1)} fusion(s32[512]{0:T(512)S(1)} %slice.141, f32[4,1024]{1,0:T(4,128)S(1)} %bitcast.45, pred[512]{0:T(512)(128)(4,1)S(1)} %iota_compare_fusion.34, f32[200,512]{1,0:T(8,128)S(1)} %collective-permute-done.4, f32[1024,200]{0,1:T(8,128)S(1)} %divide_subtract_fusion.1), kind=kOutput, calls=%fused_computation.16 | convolution fusion | flops 635961344 | bytes 3344896 | tf_op jit(solution)/shard_map/dot_general | solution.py:26
  112.5 1.2 fusion.71
  113.7 0.2 collective-permute-start.5
  113.9 1.6 %collective-permute-done.5 = f32[200,512]{1,0:T(8,128)S(1)} collective-permute-done((f32[200,512]{1,0:T(8,128)S(1)}, f32[200,512]{1,0:T(8,128)S(1)}, u32[]{:S(2)}, u32[]{:S(2)}) %collective-permute-start.5) | collective-permute-done | bytes 409632 | tf_op jit(solution)/shard_map/ppermute | solution.py:22
  115.5 0.2 multiply_add_fusion
  115.7 1.4 fusion.20.grad_ref
  117.2 36.9 %shard_map.103 = f32[1536,256]{1,0:T(8,128)S(1)} custom-call(f32[1536,256]{1,0:T(8,128)S(1)} %shard_map.102.table_ref, f32[1536,256]{1,0:T(8,128)S(1)} %fusion.20.grad_ref), custom_call_target="tpu_custom_call" | custom-call | tf_op jit(solution)/shard_map/pallas_call | solution.py:125
  154.0 1.1 slice_reduce_fusion
  155.2 0.9 fusion.12
  156.1 0.9 multiply_reduce_fusion
  157.0 0.6 fusion.67
  157.6 1.4 copy.15
  159.0 1.0 divide_subtract_fusion
  (36 shorter events, 0.9 us)
Async XLA Ops:
  0.6 11.6 %copy-start.2 = (f32[1024,200]{0,1:T(8,128)S(1)}, f32[1024,200]{0,1:T(8,128)}, u32[]{:S(2)}) copy-start(f32[1024,200]{0,1:T(8,128)} %param.7) | copy-start | bytes 2457604
  4.3 13.6 %collective-permute-start = (s32[4513]{0:T(1024)S(1)}, s32[4513]{0:T(1024)S(1)}, u32[]{:S(2)}, u32[]{:S(2)}) collective-permute-start(s32[4513]{0:T(1024)S(1)} %concatenate.27), channel_id=1, source_target_pairs={{0,16},{16,0},{1,17},{17,1},{2,18},{18,2},{3,19},{19,3},{4,20},{20... | collective-permute-start | bytes 54164 | tf_op jit(solution)/shard_map/ppermute | solution.py:22
  13.2 3.7 %copy-start.3 = (f32[200,512]{1,0:T(8,128)}, f32[200,512]{1,0:T(8,128)S(1)}, u32[]{:S(2)}) copy-start(f32[200,512]{1,0:T(8,128)S(1)} %fusion.27) | copy-start | bytes 1228804
  17.0 0.8 copy-start.5
  17.8 20.7 %collective-permute-start.1 = (f32[200,512]{1,0:T(8,128)S(1)}, f32[200,512]{1,0:T(8,128)S(1)}, u32[]{:S(2)}, u32[]{:S(2)}) collective-permute-start(f32[200,512]{1,0:T(8,128)S(1)} %pad_maximum_fusion), channel_id=1, source_target_pairs={{0,16},{16,0},{1,17},{17,1},{2,18},{18,2},{3,19},{19,3},{4,20},{20... | collective-permute-start | bytes 1228808 | tf_op jit(solution)/shard_map/ppermute | solution.py:22
  40.4 1.3 copy-start
  41.8 21.9 %copy-start.4 = (f32[200,512]{1,0:T(8,128)S(1)}, f32[200,512]{1,0:T(8,128)}, u32[]{:S(2)}) copy-start(f32[200,512]{1,0:T(8,128)} %copy-done.3) | copy-start | bytes 1228804
  43.7 19.9 %collective-permute-start.2 = (f32[200,512]{1,0:T(8,128)}, f32[200,512]{1,0:T(8,128)}, u32[]{:S(2)}, u32[]{:S(2)}) collective-permute-start(f32[200,512]{1,0:T(8,128)} %convolution_bitcast_fusion), channel_id=1, source_target_pairs={{0,16},{16,0},{1,17},{17,1},{2,18},{18,2},{3,19},{19,3},{4,20},{20... | collective-permute-start | bytes 1228808 | tf_op jit(solution)/shard_map/ppermute | solution.py:22
  44.5 1.2 collective-permute-start.3
  66.5 36.6 %copy-start.1 = (f32[512,1024]{1,0:T(8,128)S(1)}, f32[512,1024]{1,0:T(8,128)}, u32[]{:S(2)}) copy-start(f32[512,1024]{1,0:T(8,128)} %copy-done) | copy-start | bytes 6291460
  103.2 0.9 copy-start.6
  107.4 3.2 %collective-permute-start.4 = (f32[200,512]{1,0:T(8,128)S(1)}, f32[200,512]{1,0:T(8,128)S(1)}, u32[]{:S(2)}, u32[]{:S(2)}) collective-permute-start(f32[200,512]{1,0:T(8,128)S(1)} %pad_maximum_fusion.1), channel_id=1, source_target_pairs={{0,1},{1,0},{2,3},{3,2},{4,5},{5,4},{6,7},{7,6},{8,9},{9,8},{10,11... | collective-permute-start | bytes 1228808 | tf_op jit(solution)/shard_map/ppermute | solution.py:22
  113.7 1.8 %collective-permute-start.5 = (f32[200,512]{1,0:T(8,128)S(1)}, f32[200,512]{1,0:T(8,128)S(1)}, u32[]{:S(2)}, u32[]{:S(2)}) collective-permute-start(f32[200,512]{1,0:T(8,128)S(1)} %fusion.71), channel_id=1, source_target_pairs={{0,1},{1,0},{2,3},{3,2},{4,5},{5,4},{6,7},{7,6},{8,9},{9,8},{10,11... | collective-permute-start | bytes 1228808 | tf_op jit(solution)/shard_map/ppermute | solution.py:22
